TPU v7x, 32 devices: a whole 2x2x4 slice. The times are simulated.
32 devices in a mesh: strip: 8 (over z, x), col: 4 (over y, core).
Axes of the slice: x: 2, y: 2, z: 4, core: 2. Of those that a mesh axis runs over, the one named last changes fastest.
Arguments:
- net_box: int32 [32768, 4], P(('strip', 'col')), may hold values from 0 to 1023, as said below
- net_weight: float32 [32768], P(('strip', 'col')), may hold values from 0.5 to 2
- pin_bin: int32 [32768, 4, 2], P(('strip', 'col')), may hold values from 0 to 1023, as said below
- conv_first: bfloat16 [3, 3, 32, 3], replicated, may hold values from -1.25 to 1.25
- bias_first: float32 [32], replicated, may hold values from -3 to 3
- conv_second: bfloat16 [3, 3, 32, 32], replicated, may hold values from -0.375 to 0.375
- bias_second: float32 [32], replicated, may hold values from -3 to 3
- cotangent: bfloat16 [512, 32, 1024], P('col', None, 'strip'), may hold values from -6 to 6
Outputs:
- congestion: bfloat16 [512, 32, 1024], P('col', None, 'strip')
- net_grad: float32 [32768], P(('strip', 'col'))
Inputs may be any that keep to these rules, and one draw needn't show every extreme that they name: `net_box`: box n = (x0, x1, y0, y1) has x0 <= x1 < x0 + 16 and y0 <= y1 < y0 + 16; y0 lies in rows s * 128 to (s + 1) * 128 - 1, where s = n // 4096 is the strip whose devices hold net n. Some box is 16 bins tall and wide. `pin_bin`: every pin of net n lies in net n's box.
All inputs are finite; a program needn't handle non-finite values.
Results may differ from a plain program's by a relative error of at most 0.0054.
Values may be sent and summed in bfloat16 or wider, within the bound.
No kernel may reach another device: no remote copies, remote signals or barrier semaphores. Data moves between devices by JAX's collectives and lax.ppermute only.
A program may use at most 192 MiB of HBM per device.

v0:
```python
import math
import jax
import jax.numpy as jnp
from jax import lax
from jax.sharding import PartitionSpec as P


def from_behind(x, axis, by):
    size = lax.axis_size(axis)
    pairs = [(i, i + by) for i in range(size) if 0 <= i + by < size]
    return lax.ppermute(x, axis, pairs)


def with_halo(block, sides, width):
    for axis, dim in sides:
        count = lax.axis_size(axis)
        forward = [(i, i + 1) for i in range(count - 1)]
        backward = [(target, source) for source, target in forward]
        low = lax.ppermute(
            lax.slice_in_dim(block, block.shape[dim] - width, None, axis=dim), axis, forward
        )
        high = lax.ppermute(lax.slice_in_dim(block, 0, width, axis=dim), axis, backward)
        block = jnp.concatenate([low, block, high], axis=dim)
    return block


def silu_slope(pre_act):
    sigmoid = jax.nn.sigmoid(pre_act)
    return sigmoid * (1.0 + pre_act * (1.0 - sigmoid))


def conv_valid(padded, weights, out_cols, out_rows):
    summed = None
    for shift_row in range(3):
        for shift_col in range(3):
            window = padded[shift_col : shift_col + out_cols, :, shift_row : shift_row + out_rows]
            product = jnp.einsum(
                "oi,xiy->xoy",
                weights[shift_row, shift_col],
                window,
                preferred_element_type=jnp.float32,
            )
            summed = product if summed is None else summed + product
    return summed


def conv_back(padded, weights, out_cols, out_rows):
    summed = None
    for shift_row in range(3):
        for shift_col in range(3):
            window = padded[
                2 - shift_col : 2 - shift_col + out_cols,
                :,
                2 - shift_row : 2 - shift_row + out_rows,
            ]
            product = jnp.einsum(
                "oi,xoy->xiy",
                weights[shift_row, shift_col],
                window,
                preferred_element_type=jnp.float32,
            )
            summed = product if summed is None else summed + product
    return summed


def strip_factors(box_rows, weights, pin_list, first_row, span):
    row_ids = first_row + jnp.arange(2 * span, dtype=jnp.int32)
    top_row = box_rows[:, 2]
    bottom_row = box_rows[:, 3]
    inside = (top_row[:, None] <= row_ids[None, :]) & (row_ids[None, :] <= bottom_row[:, None])
    box_height = (bottom_row - top_row + 1).astype(jnp.float32)
    box_width = (box_rows[:, 1] - box_rows[:, 0] + 1).astype(jnp.float32)
    values = jnp.stack([weights / box_height, weights / box_width], axis=1).astype(jnp.bfloat16)
    row_factor = inside.astype(jnp.bfloat16).reshape(-1, 2, 1, span) * values[:, None, :, None]
    pin_rows = pin_list[:, :, 0].reshape(-1)
    pin_factor = (pin_rows[:, None] == row_ids[None, :]).astype(jnp.bfloat16).reshape(-1, 2, span)
    return (row_factor, pin_list[:, :, 1].reshape(-1), pin_factor)


def column_block(col_ids, left_col, right_col, row_factor, pin_col, pin_factor):
    net_cols = (
        (left_col[:, None] <= col_ids[None, :]) & (col_ids[None, :] <= right_col[:, None])
    ).astype(jnp.bfloat16)
    pin_cols = (pin_col[:, None] == col_ids[None, :]).astype(jnp.bfloat16)
    demand = jnp.einsum("nk,nhcr->khcr", net_cols, row_factor, preferred_element_type=jnp.float32)
    density = jnp.einsum("pk,phr->khr", pin_cols, pin_factor, preferred_element_type=jnp.float32)
    return jnp.concatenate([demand, density[:, :, None, :]], axis=2)


def shards(
    net_box, net_weight, pin_bin, conv_first, bias_first, conv_second, bias_second, cotangent
):
    tile_cols = cotangent.shape[0]
    span = cotangent.shape[2]
    net_total = net_box.shape[0]
    strip_index = lax.axis_index("strip")
    col_index = lax.axis_index("col")
    all_rows = span * lax.axis_size("strip")
    all_cols = tile_cols * lax.axis_size("col")
    first_row = strip_index * span
    pin_width = pin_bin.shape[1]
    packed = jnp.concatenate(
        [
            net_box.astype(jnp.float32),
            pin_bin.reshape(net_total, 2 * pin_width).astype(jnp.float32),
            net_weight[:, None],
        ],
        axis=1,
    )
    own_cols = col_index * tile_cols + jnp.arange(tile_cols, dtype=jnp.int32)
    start_terms = jnp.zeros((tile_cols, 2, 3, span), jnp.float32)
    shard_piece = lax.all_gather(packed, "col", axis=0, tiled=True)
    piece_rows = shard_piece.shape[0]
    block_size = math.gcd(piece_rows, 1024)
    grouped = shard_piece.reshape(piece_rows // block_size, block_size, shard_piece.shape[1])

    def one_group(summed, net_group):
        box_rows = net_group[:, :4].astype(jnp.int32)
        pin_list = (
            net_group[:, 4 : 4 + 2 * pin_width].reshape(block_size, pin_width, 2).astype(jnp.int32)
        )
        weights = net_group[:, 4 + 2 * pin_width]
        row_factor, pin_col, pin_factor = strip_factors(
            box_rows, weights, pin_list, first_row, span
        )
        return (
            summed
            + column_block(
                own_cols, box_rows[:, 0], box_rows[:, 1], row_factor, pin_col, pin_factor
            ),
            None,
        )

    summed, unused = lax.scan(one_group, start_terms, grouped)
    spilled = from_behind(summed[:, 1].astype(jnp.bfloat16), "strip", 1).astype(jnp.float32)
    features = (summed[:, 0] + spilled).astype(jnp.bfloat16)
    stacked = jnp.concatenate([features, cotangent], axis=1)
    padded = with_halo(stacked, (("strip", 2), ("col", 0)), 2)
    in_channels = features.shape[1]
    col_ids = col_index * tile_cols - 1 + jnp.arange(tile_cols + 2, dtype=jnp.int32)
    row_ids = first_row - 1 + jnp.arange(span + 2, dtype=jnp.int32)
    inside = ((col_ids >= 0) & (col_ids < all_cols))[:, None, None] & (
        (row_ids >= 0) & (row_ids < all_rows)
    )[None, None, :]
    pre_act = (
        conv_valid(padded[:, :in_channels], conv_first, tile_cols + 2, span + 2)
        + bias_first[None, :, None]
    )
    hidden = jnp.where(inside, jax.nn.silu(pre_act), 0.0).astype(jnp.bfloat16)
    congestion = (
        conv_valid(hidden, conv_second, tile_cols, span) + bias_second[None, :, None]
    ).astype(jnp.bfloat16)
    back_hidden = conv_back(padded[:, in_channels:], conv_second, tile_cols + 2, span + 2)
    back_pre = jnp.where(inside, back_hidden * silu_slope(pre_act), 0.0).astype(jnp.bfloat16)
    back_maps = conv_back(back_pre, conv_first[:, :, :, :2], tile_cols, span).astype(jnp.bfloat16)
    from_below = from_behind(back_maps, "strip", -1)
    both_halves = jnp.stack([back_maps, from_below], axis=1).reshape(tile_cols, 4 * span)
    left_col = net_box[:, 0]
    right_col = net_box[:, 1]
    shard_piece = lax.all_gather(both_halves, "col", axis=0, tiled=True)
    piece_cols = jnp.arange(shard_piece.shape[0], dtype=jnp.int32)
    net_cols = (
        (left_col[:, None] <= piece_cols[None, :]) & (piece_cols[None, :] <= right_col[:, None])
    ).astype(jnp.bfloat16)
    column_sums = jnp.dot(net_cols, shard_piece, preferred_element_type=jnp.float32)
    column_sums = column_sums.reshape(net_total, 2, 2, span)
    net_rows = first_row + jnp.arange(2 * span, dtype=jnp.int32)
    in_rows = (
        (
            (net_box[:, 2][:, None] <= net_rows[None, :])
            & (net_rows[None, :] <= net_box[:, 3][:, None])
        )
        .astype(jnp.float32)
        .reshape(net_total, 2, span)
    )
    box_height = (net_box[:, 3] - net_box[:, 2] + 1).astype(jnp.float32)
    box_width = (right_col - left_col + 1).astype(jnp.float32)
    per_row = (
        column_sums[:, :, 0] / box_height[:, None, None]
        + column_sums[:, :, 1] / box_width[:, None, None]
    )
    net_grad = jnp.sum(in_rows * per_row, axis=(1, 2))
    return (congestion, net_grad)


def solution(mesh):
    placed = (
        P(("strip", "col"), None),
        P(("strip", "col")),
        P(("strip", "col"), None, None),
        P(),
        P(),
        P(),
        P(),
        P("col", None, "strip"),
    )
    return jax.shard_map(
        shards,
        mesh=mesh,
        in_specs=placed,
        out_specs=(P("col", None, "strip"), P(("strip", "col"))),
        check_vma=False,
    )
```

profile of v0, /device:TPU:19, one launch (start us, length us, event | category | flops | bytes accessed | tf_op | source)
XLA Modules:
  0.0 179.9 jit_solution(665664036078959381)
XLA Ops:
  0.6 0.8 convert_element_type.81
  1.5 0.7 convert_element_type.80
  2.2 0.7 pad_maximum_fusion.10
  2.9 6.3 %all_gather.6 = f32[4096,13]{0,1:T(8,128)S(1)} all-gather(f32[1024,13]{0,1:T(8,128)S(1)} %pad_maximum_fusion.10), channel_id=1, replica_groups=mesh['strip'=8,'col'=4] {'col'}, dimensions={0}, use_global_device_ids=true | all-gather | bytes 266240 | tf_op jit(solution)/shard_map/all_gather | solution.py:112
  9.4 13.7 %while.11 = (s32[]{:T(128)}, f32[128,2,3,128]{3,0,2,1:T(8,128)S(1)}, f32[4,1024,13]{1,0,2:T(4,128)S(1)}, s32[]{:T(128)}, s32[]{:T(128)}, /*index=5*/s32[]{:T(128)}, s32[]{:T(128)}) while((s32[]{:T(128)}, f32[128,2,3,128]{3,0,2,1:T(8,128)S(1)}, f32[4,1024,13]{1,0,2:T(4,128)S(1)}, s32[]{:T(128)}, s32[]{:T(128)}, ...), condition=%wide.region_1.2_spmd.clone, body=%wide.region_0.1_spmd.clone.sunk | while | flops 408091520 | bytes 3318379 | solution.py:134
  10.6 1.1 fusion.251
  12.1 0.5 fusion.254
  14.0 1.1 fusion.251
  15.5 0.5 fusion.254
  17.4 1.1 fusion.251
  19.0 0.5 fusion.254
  20.9 1.1 fusion.251
  22.4 0.5 fusion.254
  23.3 3.2 %collective-permute-start = (bf16[128,3,128]{0,2,1:T(8,128)(2,1)S(1)}, bf16[128,3,128]{0,2,1:T(8,128)(2,1)S(1)}, u32[]{:S(2)}, u32[]{:S(2)}) collective-permute-start(bf16[128,3,128]{0,2,1:T(8,128)(2,1)S(1)} %fusion.144), channel_id=1, source_target_pairs={{0,4},{4,8},{8,12},{12,16},{16,20},{20,24},{24,28},{1,5},{5,9},{9,... | collective-permute-start | bytes 294920 | tf_op jit(solution)/shard_map/ppermute | solution.py:11
  26.6 1.0 copy.57
  27.6 1.8 %collective-permute-done = bf16[128,3,128]{0,2,1:T(8,128)(2,1)S(1)} collective-permute-done((bf16[128,3,128]{0,2,1:T(8,128)(2,1)S(1)}, bf16[128,3,128]{0,2,1:T(8,128)(2,1)S(1)}, u32[]{:S(2)}, u32[]{:S(2)}) %collective-permute-start) | collective-permute-done | bytes 98336 | tf_op jit(solution)/shard_map/ppermute | solution.py:11
  29.5 3.1 %collective-permute-start.2 = (bf16[128,35,2]{0,2,1:T(2,128)(2,1)S(1)}, bf16[128,35,2]{0,2,1:T(2,128)(2,1)S(1)}, u32[]{:S(2)}, u32[]{:S(2)}) collective-permute-start(bf16[128,35,2]{0,2,1:T(2,128)(2,1)S(1)} %get-tuple-element.87), channel_id=1, source_target_pairs={{4,0},{8,4},{12,8},{16,12},{20,16},{24,20},{28,24},{5,1},{9,5},{13... | collective-permute-start | bytes 53768 | tf_op jit(solution)/shard_map/ppermute | solution.py:22
  32.6 3.1 %collective-permute-start.1 = (bf16[128,35,2]{0,2,1:T(2,128)(2,1)S(1)}, bf16[128,35,2]{0,2,1:T(2,128)(2,1)S(1)}, u32[]{:S(2)}, u32[]{:S(2)}) collective-permute-start(bf16[128,35,2]{0,2,1:T(2,128)(2,1)S(1)} %get-tuple-element.86), channel_id=1, source_target_pairs={{0,4},{4,8},{8,12},{12,16},{16,20},{20,24},{24,28},{1,5},{5,9},{9,... | collective-permute-start | bytes 53768 | tf_op jit(solution)/shard_map/ppermute | solution.py:19
  35.7 1.3 collective-permute-done.1
  37.1 1.6 pad_maximum_fusion.8
  38.7 3.6 %copy.58 = bf16[128,35,132]{2,1,0:T(8,128)(2,1)S(1)} copy(bf16[128,35,132]{0,2,1:T(8,128)(2,1)} %pad_maximum_fusion.8) | data formatting | bytes 2365440 | tf_op jit(solution)/shard_map/concatenate | solution.py:23
  42.3 5.4 %collective-permute-start.3 = (bf16[2,35,132]{2,1,0:T(8,128)(2,1)S(1)}, bf16[2,35,132]{2,1,0:T(8,128)(2,1)S(1)}, u32[]{:S(2)}, u32[]{:S(2)}) collective-permute-start(bf16[2,35,132]{2,1,0:T(8,128)(2,1)S(1)} %get-tuple-element.84), channel_id=1, source_target_pairs={{0,1},{1,2},{2,3},{4,5},{5,6},{6,7},{8,9},{9,10},{10,11},{12,13},{... | collective-permute-start | bytes 55448 | tf_op jit(solution)/shard_map/ppermute | solution.py:19
  47.8 2.1 %collective-permute-start.4 = (bf16[2,35,132]{2,1,0:T(8,128)(2,1)S(1)}, bf16[2,35,132]{2,1,0:T(8,128)(2,1)S(1)}, u32[]{:S(2)}, u32[]{:S(2)}) collective-permute-start(bf16[2,35,132]{2,1,0:T(8,128)(2,1)S(1)} %get-tuple-element.85), channel_id=1, source_target_pairs={{1,0},{2,1},{3,2},{5,4},{6,5},{7,6},{9,8},{10,9},{11,10},{13,12},{... | collective-permute-start | bytes 55448 | tf_op jit(solution)/shard_map/ppermute | solution.py:22
  49.9 2.7 %fusion.110 = f32[130,130,32]{1,2,0:T(8,128)} fusion(bf16[128,35,132]{2,1,0:T(8,128)(2,1)S(1)} %copy.58, bf16[2,35,132]{2,1,0:T(8,128)(2,1)S(1)} %collective-permute-done.3, bf16[3,3,32,3]{2,3,1,0:T(4,128)(2,1)S(1)} %copy-done.10), kind=kOutput, calls=%fused_computation.139 | convolution fusion | flops 3447600 | bytes 4826624 | tf_op jit(solution)/shard_map/oi,xiy->xoy/dot_general | solution.py:37
  53.1 2.9 %fusion.104 = f32[130,130,32]{1,2,0:T(8,128)} fusion(bf16[2,35,132]{2,1,0:T(8,128)(2,1)S(1)} %collective-permute-done.4, bf16[128,35,132]{2,1,0:T(8,128)(2,1)S(1)} %copy.58, bf16[2,35,132]{2,1,0:T(8,128)(2,1)S(1)} %collective-permute-done.3, bf16[3,3,32,3]{2,3,1,0:T(4,128)(2,1)S(1)} %copy-done.10), kind=kOutput, calls=%fused_computation.133 | convolution fusion | flops 3549000 | bytes 4867584 | tf_op jit(solution)/shard_map/oi,xiy->xoy/dot_general | solution.py:37
  56.0 2.8 %fusion.114 = f32[130,130,32]{1,2,0:T(8,128)} fusion(bf16[2,35,132]{2,1,0:T(8,128)(2,1)S(1)} %collective-permute-done.4, bf16[128,35,132]{2,1,0:T(8,128)(2,1)S(1)} %copy.58, bf16[3,3,32,3]{2,3,1,0:T(4,128)(2,1)S(1)} %copy-done.10), kind=kOutput, calls=%fused_computation.143 | convolution fusion | flops 3447600 | bytes 4826624 | tf_op jit(solution)/shard_map/oi,xiy->xoy/dot_general | solution.py:37
  58.8 2.8 %fusion.118 = f32[130,130,32]{1,2,0:T(8,128)} fusion(bf16[2,35,132]{2,1,0:T(8,128)(2,1)S(1)} %collective-permute-done.4, bf16[128,35,132]{2,1,0:T(8,128)(2,1)S(1)} %copy.58, bf16[2,35,132]{2,1,0:T(8,128)(2,1)S(1)} %collective-permute-done.3, bf16[3,3,32,3]{2,3,1,0:T(4,128)(2,1)S(1)} %copy-done.10), kind=kOutput, calls=%fused_computation.147 | convolution fusion | flops 3549000 | bytes 4867584 | tf_op jit(solution)/shard_map/oi,xiy->xoy/dot_general | solution.py:37
  61.6 2.7 %fusion.124 = f32[130,130,32]{1,2,0:T(8,128)} fusion(bf16[128,35,132]{2,1,0:T(8,128)(2,1)S(1)} %copy.58, bf16[2,35,132]{2,1,0:T(8,128)(2,1)S(1)} %collective-permute-done.3, bf16[3,3,32,3]{2,3,1,0:T(4,128)(2,1)S(1)} %copy-done.10), kind=kOutput, calls=%fused_computation.153 | convolution fusion | flops 3447600 | bytes 4826624 | tf_op jit(solution)/shard_map/oi,xiy->xoy/dot_general | solution.py:37
  64.3 2.7 %fusion.128 = f32[130,130,32]{1,2,0:T(8,128)} fusion(bf16[2,35,132]{2,1,0:T(8,128)(2,1)S(1)} %collective-permute-done.4, bf16[128,35,132]{2,1,0:T(8,128)(2,1)S(1)} %copy.58, bf16[3,3,32,3]{2,3,1,0:T(4,128)(2,1)S(1)} %copy-done.10), kind=kOutput, calls=%fused_computation.157 | convolution fusion | flops 3447600 | bytes 4826624 | tf_op jit(solution)/shard_map/oi,xiy->xoy/dot_general | solution.py:37
  67.0 2.8 %fusion.138 = f32[130,130,32]{1,2,0:T(8,128)} fusion(bf16[128,35,132]{2,1,0:T(8,128)(2,1)S(1)} %copy.58, bf16[2,35,132]{2,1,0:T(8,128)(2,1)S(1)} %collective-permute-done.3, bf16[3,3,32,3]{2,3,1,0:T(4,128)(2,1)S(1)} %copy-done.10), kind=kOutput, calls=%fused_computation.167 | convolution fusion | flops 3447600 | bytes 4826624 | tf_op jit(solution)/shard_map/oi,xiy->xoy/dot_general | solution.py:37
  69.8 2.8 %fusion.132 = f32[130,130,32]{1,2,0:T(8,128)} fusion(bf16[2,35,132]{2,1,0:T(8,128)(2,1)S(1)} %collective-permute-done.4, bf16[128,35,132]{2,1,0:T(8,128)(2,1)S(1)} %copy.58, bf16[2,35,132]{2,1,0:T(8,128)(2,1)S(1)} %collective-permute-done.3, bf16[3,3,32,3]{2,3,1,0:T(4,128)(2,1)S(1)} %copy-done.10), kind=kOutput, calls=%fused_computation.161 | convolution fusion | flops 3549000 | bytes 4867584 | tf_op jit(solution)/shard_map/oi,xiy->xoy/dot_general | solution.py:37
  72.6 14.8 %fusion.34 = (bf16[130,32,130]{2,1,0:T(8,128)(2,1)S(1)}, f32[130,130,32]{1,2,0:T(8,128)}) fusion(pred[130,130]{1,0:T(8,128)(4,1)S(1)} %broadcast_and_fusion, f32[32]{0:T(128)S(1)} %copy-done.12, bf16[3,3,32,3]{2,3,1,0:T(4,128)(2,1)S(1)} %copy-done.10, bf16[2,35,132]{2,1,0:T(8,128)(2,1)S(1)} %collective-permute-done.4, bf16[128,35,132]{2,1,0:T(8,128)(2,1)S(1)} %copy.58, ...), kind=kOutput, calls=%fused_computation.44 | convolution fusion | flops 11559600 | bytes 23249152 | tf_op jit(solution)/shard_map/oi,xiy->xoy/dot_general | solution.py:37
  87.5 1.9 %fusion.79 = f32[128,128,32]{1,2,0:T(8,128)} fusion(bf16[130,32,130]{2,1,0:T(8,128)(2,1)S(1)} %get-tuple-element.92, bf16[3,3,32,32]{3,2,1,0:T(8,128)(2,1)S(1)} %copy-done.8), kind=kOutput, calls=%fused_computation.110 | convolution fusion | flops 33554432 | bytes 3153920 | tf_op jit(solution)/shard_map/oi,xiy->xoy/dot_general | solution.py:37
  89.4 1.9 %fusion.81 = f32[128,128,32]{1,2,0:T(8,128)} fusion(bf16[130,32,130]{2,1,0:T(8,128)(2,1)S(1)} %get-tuple-element.92, bf16[3,3,32,32]{3,2,1,0:T(8,128)(2,1)S(1)} %copy-done.8), kind=kOutput, calls=%fused_computation.112 | convolution fusion | flops 33554432 | bytes 3153920 | tf_op jit(solution)/shard_map/oi,xiy->xoy/dot_general | solution.py:37
  91.2 1.9 %fusion.83 = f32[128,128,32]{1,2,0:T(8,128)} fusion(bf16[130,32,130]{2,1,0:T(8,128)(2,1)S(1)} %get-tuple-element.92, bf16[3,3,32,32]{3,2,1,0:T(8,128)(2,1)S(1)} %copy-done.8), kind=kOutput, calls=%fused_computation.114 | convolution fusion | flops 33554432 | bytes 3153920 | tf_op jit(solution)/shard_map/oi,xiy->xoy/dot_general | solution.py:37
  93.1 1.8 %fusion.85 = f32[128,128,32]{1,2,0:T(8,128)} fusion(bf16[130,32,130]{2,1,0:T(8,128)(2,1)S(1)} %get-tuple-element.92, bf16[3,3,32,32]{3,2,1,0:T(8,128)(2,1)S(1)} %copy-done.8), kind=kOutput, calls=%fused_computation.116 | convolution fusion | flops 33554432 | bytes 3153920 | tf_op jit(solution)/shard_map/oi,xiy->xoy/dot_general | solution.py:37
  95.0 1.8 %fusion.87 = f32[128,128,32]{1,2,0:T(8,128)} fusion(bf16[130,32,130]{2,1,0:T(8,128)(2,1)S(1)} %get-tuple-element.92, bf16[3,3,32,32]{3,2,1,0:T(8,128)(2,1)S(1)} %copy-done.8), kind=kOutput, calls=%fused_computation.118 | convolution fusion | flops 33554432 | bytes 3153920 | tf_op jit(solution)/shard_map/oi,xiy->xoy/dot_general | solution.py:37
  96.8 1.8 fusion.89
  98.6 1.7 fusion.93
  100.3 1.7 fusion.91
  102.0 0.6 pad_maximum_fusion.1
  102.6 2.7 %fusion.51 = f32[130,130,32]{1,2,0:T(8,128)} fusion(bf16[132,35,132]{2,1,0:T(8,128)(2,1)S(1)} %pad_maximum_fusion.1, bf16[3,3,32,32]{3,2,1,0:T(8,128)(2,1)S(1)} %copy-done.8), kind=kOutput, calls=%fused_computation.68 | convolution fusion | flops 34611200 | bytes 4301312 | tf_op jit(solution)/shard_map/oi,xoy->xiy/dot_general | solution.py:56
  105.3 3.1 %fusion.55 = f32[130,130,32]{1,2,0:T(8,128)} fusion(bf16[132,35,132]{2,1,0:T(8,128)(2,1)S(1)} %pad_maximum_fusion.1, bf16[3,3,32,32]{3,2,1,0:T(8,128)(2,1)S(1)} %copy-done.8), kind=kOutput, calls=%fused_computation.73 | convolution fusion | flops 34611200 | bytes 4301312 | tf_op jit(solution)/shard_map/oi,xoy->xiy/dot_general | solution.py:56
  108.5 3.2 %fusion.57 = f32[130,130,32]{1,2,0:T(8,128)} fusion(bf16[132,35,132]{2,1,0:T(8,128)(2,1)S(1)} %pad_maximum_fusion.1, bf16[3,3,32,32]{3,2,1,0:T(8,128)(2,1)S(1)} %copy-done.8), kind=kOutput, calls=%fused_computation.75 | convolution fusion | flops 34611200 | bytes 4301312 | tf_op jit(solution)/shard_map/oi,xoy->xiy/dot_general | solution.py:56
  111.6 2.8 %fusion.53 = f32[130,130,32]{1,2,0:T(8,128)} fusion(bf16[2,35,132]{2,1,0:T(8,128)(2,1)S(1)} %collective-permute-done.4, bf16[128,35,132]{2,1,0:T(8,128)(2,1)S(1)} %copy.58, bf16[3,3,32,32]{3,2,1,0:T(8,128)(2,1)S(1)} %copy-done.8), kind=kOutput, calls=%fused_computation.71 | convolution fusion | flops 36774400 | bytes 4833792 | tf_op jit(solution)/shard_map/oi,xoy->xiy/dot_general | solution.py:56
  114.5 3.6 %fusion.44 = f32[130,130,32]{1,2,0:T(8,128)} fusion(bf16[128,35,132]{2,1,0:T(8,128)(2,1)S(1)} %copy.58, bf16[2,35,132]{2,1,0:T(8,128)(2,1)S(1)} %collective-permute-done.3, bf16[3,3,32,32]{3,2,1,0:T(8,128)(2,1)S(1)} %copy-done.8), kind=kOutput, calls=%fused_computation.62 | convolution fusion | flops 35152000 | bytes 4833792 | tf_op jit(solution)/shard_map/oi,xoy->xiy/dot_general | solution.py:56
  118.1 3.6 %fusion.38 = f32[130,130,32]{1,2,0:T(8,128)} fusion(bf16[128,35,132]{2,1,0:T(8,128)(2,1)S(1)} %copy.58, bf16[2,35,132]{2,1,0:T(8,128)(2,1)S(1)} %collective-permute-done.4, bf16[3,3,32,32]{3,2,1,0:T(8,128)(2,1)S(1)} %copy-done.8), kind=kOutput, calls=%fused_computation.58 | convolution fusion | flops 35152000 | bytes 4833792 | tf_op jit(solution)/shard_map/oi,xoy->xiy/dot_general | solution.py:56
  121.7 3.9 %fusion.47 = f32[130,130,32]{1,2,0:T(8,128)} fusion(bf16[128,35,132]{2,1,0:T(8,128)(2,1)S(1)} %copy.58, bf16[2,35,132]{2,1,0:T(8,128)(2,1)S(1)} %collective-permute-done.3, bf16[3,3,32,32]{3,2,1,0:T(8,128)(2,1)S(1)} %copy-done.8), kind=kOutput, calls=%fused_computation.64 | convolution fusion | flops 35152000 | bytes 4833792 | tf_op jit(solution)/shard_map/oi,xoy->xiy/dot_general | solution.py:56
  125.7 3.7 %fusion.41 = f32[130,130,32]{1,2,0:T(8,128)} fusion(bf16[128,35,132]{2,1,0:T(8,128)(2,1)S(1)} %copy.58, bf16[2,35,132]{2,1,0:T(8,128)(2,1)S(1)} %collective-permute-done.4, bf16[3,3,32,32]{3,2,1,0:T(8,128)(2,1)S(1)} %copy-done.8), kind=kOutput, calls=%fused_computation.60 | convolution fusion | flops 35152000 | bytes 4833792 | tf_op jit(solution)/shard_map/oi,xoy->xiy/dot_general | solution.py:56
  129.4 15.3 %fusion.29 = bf16[130,32,130]{2,1,0:T(8,128)(2,1)} fusion(f32[130,130,32]{1,2,0:T(8,128)} %get-tuple-element.93, f32[130,130,32]{1,2,0:T(8,128)} %fusion.51, f32[130,130,32]{1,2,0:T(8,128)} %fusion.53, f32[130,130,32]{1,2,0:T(8,128)} %fusion.44, f32[130,130,32]{1,2,0:T(8,128)} %fusion.55, f32[130,130,32]{1,2,0:T(8,128)} %fusion.38, ...), kind=kOutput, calls=%fused_computation.36 | convolution fusion | flops 46508800 | bytes 23255808 | tf_op jit(solution)/shard_map/oi,xoy->xiy/dot_general | solution.py:56
  144.7 2.1 %fusion.76 = f32[128,128,2]{1,2,0:T(2,128)S(1)} fusion(bf16[130,32,130]{2,1,0:T(8,128)(2,1)} %fusion.29, bf16[3,3,32,3]{2,3,1,0:T(4,128)(2,1)S(1)} %copy-done.10), kind=kOutput, calls=%fused_computation.107 | convolution fusion | flops 2097152 | bytes 1180160 | tf_op jit(solution)/shard_map/oi,xoy->xiy/dot_general | solution.py:56
  146.8 2.2 %convolution_add_fusion.7 = f32[128,128,2]{1,2,0:T(2,128)S(1)} fusion(f32[128,128,2]{1,2,0:T(2,128)S(1)} %fusion.76, bf16[130,32,130]{2,1,0:T(8,128)(2,1)} %fusion.29, bf16[3,3,32,3]{2,3,1,0:T(4,128)(2,1)S(1)} %copy-done.10), kind=kOutput, calls=%fused_computation.91 | convolution fusion | flops 2129920 | bytes 1311232 | tf_op jit(solution)/shard_map/oi,xoy->xiy/dot_general | solution.py:56
  149.0 2.2 %convolution_add_fusion.6 = f32[128,128,2]{1,2,0:T(2,128)S(1)} fusion(f32[128,128,2]{1,2,0:T(2,128)S(1)} %convolution_add_fusion.7, bf16[130,32,130]{2,1,0:T(8,128)(2,1)} %fusion.29, bf16[3,3,32,3]{2,3,1,0:T(4,128)(2,1)S(1)} %copy-done.10), kind=kOutput, calls=%fused_computation.90 | convolution fusion | flops 2129920 | bytes 1311232 | tf_op jit(solution)/shard_map/oi,xoy->xiy/dot_general | solution.py:56
  151.3 2.1 %convolution_add_fusion.5 = f32[128,128,2]{1,2,0:T(2,128)S(1)} fusion(f32[128,128,2]{1,2,0:T(2,128)S(1)} %convolution_add_fusion.6, bf16[130,32,130]{2,1,0:T(8,128)(2,1)} %fusion.29, bf16[3,3,32,3]{2,3,1,0:T(4,128)(2,1)S(1)} %copy-done.10), kind=kOutput, calls=%fused_computation.89 | convolution fusion | flops 2129920 | bytes 1311232 | tf_op jit(solution)/shard_map/oi,xoy->xiy/dot_general | solution.py:56
  153.4 2.2 %convolution_add_fusion.4 = f32[128,128,2]{1,2,0:T(2,128)S(1)} fusion(f32[128,128,2]{1,2,0:T(2,128)S(1)} %convolution_add_fusion.5, bf16[130,32,130]{2,1,0:T(8,128)(2,1)} %fusion.29, bf16[3,3,32,3]{2,3,1,0:T(4,128)(2,1)S(1)} %copy-done.10), kind=kOutput, calls=%fused_computation.88 | convolution fusion | flops 2129920 | bytes 1311232 | tf_op jit(solution)/shard_map/oi,xoy->xiy/dot_general | solution.py:56
  155.6 2.2 %convolution_add_fusion.3 = f32[128,128,2]{1,2,0:T(2,128)S(1)} fusion(f32[128,128,2]{1,2,0:T(2,128)S(1)} %convolution_add_fusion.4, bf16[130,32,130]{2,1,0:T(8,128)(2,1)} %fusion.29, bf16[3,3,32,3]{2,3,1,0:T(4,128)(2,1)S(1)} %copy-done.10), kind=kOutput, calls=%fused_computation.87 | convolution fusion | flops 2129920 | bytes 1311232 | tf_op jit(solution)/shard_map/oi,xoy->xiy/dot_general | solution.py:56
  157.9 1.5 convolution_add_fusion.2
  159.4 1.5 convolution_add_fusion.1
  160.8 1.5 fusion.63
  162.3 3.0 %collective-permute-start.5 = (bf16[128,2,128]{2,1,0:T(2,128)(2,1)S(1)}, bf16[128,2,128]{2,1,0:T(2,128)(2,1)S(1)}, u32[]{:S(2)}, u32[]{:S(2)}) collective-permute-start(bf16[128,2,128]{2,1,0:T(2,128)(2,1)S(1)} %bitcast.290), channel_id=1, source_target_pairs={{4,0},{8,4},{12,8},{16,12},{20,16},{24,20},{28,24},{5,1},{9,5},{13... | collective-permute-start | bytes 196616 | tf_op jit(solution)/shard_map/ppermute | solution.py:11
  165.4 4.2 %fusion.62 = bf16[128,32,128]{2,1,0:T(8,128)(2,1)} fusion(f32[128,128,32]{1,2,0:T(8,128)S(1)} %copy-done, f32[128,128,32]{1,2,0:T(8,128)S(1)} %copy-done.1, f32[128,128,32]{1,2,0:T(8,128)S(1)} %copy-done.2, f32[128,128,32]{1,2,0:T(8,128)S(1)} %copy-done.3, f32[128,128,32]{1,2,0:T(8,128)S(1)} %copy-done.4, f32[128,128,32]{1,2,0:T(8,128)S(1)} %copy-done.5, ...), kind=kOutput, calls=%fused_computation.82 | convolution fusion | flops 38797312 | bytes 18883072 | tf_op jit(solution)/shard_map/oi,xiy->xoy/dot_general | solution.py:37
  169.9 7.5 %all_gather.7 = bf16[512,512]{0,1:T(8,128)(2,1)S(1)} all-gather(bf16[128,512]{0,1:T(8,128)(2,1)S(1)} %bitcast.285), channel_id=1, replica_groups=mesh['strip'=8,'col'=4] {'col'}, dimensions={0}, use_global_device_ids=true | all-gather | bytes 655360 | tf_op jit(solution)/shard_map/all_gather | solution.py:160
  177.4 1.5 fusion.60
  179.0 0.9 fusion.97
  (113 shorter events, 8.0 us)
Async XLA Ops:
  9.3 17.3 %copy-start.9 = (s32[1024,4]{0,1:T(4,128)S(1)}, s32[1024,4]{0,1:T(4,128)}, u32[]{:S(2)}) copy-start(s32[1024,4]{0,1:T(4,128)} %param.10) | copy-start | bytes 49156
  9.3 17.3 %copy-start.7 = (bf16[128,32,128]{2,1,0:T(8,128)(2,1)S(1)}, bf16[128,32,128]{2,1,0:T(8,128)(2,1)}, u32[]{:S(2)}) copy-start(bf16[128,32,128]{2,1,0:T(8,128)(2,1)} %param.17) | copy-start | bytes 3145732
  23.3 6.1 %collective-permute-start = (bf16[128,3,128]{0,2,1:T(8,128)(2,1)S(1)}, bf16[128,3,128]{0,2,1:T(8,128)(2,1)S(1)}, u32[]{:S(2)}, u32[]{:S(2)}) collective-permute-start(bf16[128,3,128]{0,2,1:T(8,128)(2,1)S(1)} %fusion.144), channel_id=1, source_target_pairs={{0,4},{4,8},{8,12},{12,16},{16,20},{20,24},{24,28},{1,5},{5,9},{9,... | collective-permute-start | bytes 294920 | tf_op jit(solution)/shard_map/ppermute | solution.py:11
  29.5 6.2 %collective-permute-start.2 = (bf16[128,35,2]{0,2,1:T(2,128)(2,1)S(1)}, bf16[128,35,2]{0,2,1:T(2,128)(2,1)S(1)}, u32[]{:S(2)}, u32[]{:S(2)}) collective-permute-start(bf16[128,35,2]{0,2,1:T(2,128)(2,1)S(1)} %get-tuple-element.87), channel_id=1, source_target_pairs={{4,0},{8,4},{12,8},{16,12},{20,16},{24,20},{28,24},{5,1},{9,5},{13... | collective-permute-start | bytes 53768 | tf_op jit(solution)/shard_map/ppermute | solution.py:22
  32.6 4.5 %collective-permute-start.1 = (bf16[128,35,2]{0,2,1:T(2,128)(2,1)S(1)}, bf16[128,35,2]{0,2,1:T(2,128)(2,1)S(1)}, u32[]{:S(2)}, u32[]{:S(2)}) collective-permute-start(bf16[128,35,2]{0,2,1:T(2,128)(2,1)S(1)} %get-tuple-element.86), channel_id=1, source_target_pairs={{0,4},{4,8},{8,12},{12,16},{16,20},{20,24},{24,28},{1,5},{5,9},{9,... | collective-permute-start | bytes 53768 | tf_op jit(solution)/shard_map/ppermute | solution.py:19
  35.7 14.2 %copy-start.10 = (bf16[3,3,32,3]{2,3,1,0:T(4,128)(2,1)S(1)}, bf16[3,3,32,3]{2,3,1,0:T(4,128)(2,1)}, u32[]{:S(2)}) copy-start(bf16[3,3,32,3]{2,3,1,0:T(4,128)(2,1)} %param.13) | copy-start | bytes 5188
  42.3 7.6 %collective-permute-start.3 = (bf16[2,35,132]{2,1,0:T(8,128)(2,1)S(1)}, bf16[2,35,132]{2,1,0:T(8,128)(2,1)S(1)}, u32[]{:S(2)}, u32[]{:S(2)}) collective-permute-start(bf16[2,35,132]{2,1,0:T(8,128)(2,1)S(1)} %get-tuple-element.84), channel_id=1, source_target_pairs={{0,1},{1,2},{2,3},{4,5},{5,6},{6,7},{8,9},{9,10},{10,11},{12,13},{... | collective-permute-start | bytes 55448 | tf_op jit(solution)/shard_map/ppermute | solution.py:19
  47.8 5.3 %collective-permute-start.4 = (bf16[2,35,132]{2,1,0:T(8,128)(2,1)S(1)}, bf16[2,35,132]{2,1,0:T(8,128)(2,1)S(1)}, u32[]{:S(2)}, u32[]{:S(2)}) collective-permute-start(bf16[2,35,132]{2,1,0:T(8,128)(2,1)S(1)} %get-tuple-element.85), channel_id=1, source_target_pairs={{1,0},{2,1},{3,2},{5,4},{6,5},{7,6},{9,8},{10,9},{11,10},{13,12},{... | collective-permute-start | bytes 55448 | tf_op jit(solution)/shard_map/ppermute | solution.py:22
  69.8 2.8 %copy-start.12 = (f32[32]{0:T(128)S(1)}, f32[32]{0:T(128)}, u32[]{:S(2)}) copy-start(f32[32]{0:T(128)} %param.14) | copy-start | bytes 388
  72.6 14.8 %copy-start.8 = (bf16[3,3,32,32]{3,2,1,0:T(8,128)(2,1)S(1)}, bf16[3,3,32,32]{3,2,1,0:T(8,128)(2,1)}, u32[]{:S(2)}) copy-start(bf16[3,3,32,32]{3,2,1,0:T(8,128)(2,1)} %param.15) | copy-start | bytes 55300
  129.4 36.0 %copy-start.5 = (f32[128,128,32]{1,2,0:T(8,128)S(1)}, f32[128,128,32]{1,2,0:T(8,128)}, u32[]{:S(2)}) copy-start(f32[128,128,32]{1,2,0:T(8,128)} %fusion.89) | copy-start | bytes 6291460
  129.4 36.0 %copy-start.6 = (f32[128,128,32]{1,2,0:T(8,128)S(1)}, f32[128,128,32]{1,2,0:T(8,128)}, u32[]{:S(2)}) copy-start(f32[128,128,32]{1,2,0:T(8,128)} %fusion.93) | copy-start | bytes 6291460
  146.8 18.6 %copy-start.4 = (f32[128,128,32]{1,2,0:T(8,128)S(1)}, f32[128,128,32]{1,2,0:T(8,128)}, u32[]{:S(2)}) copy-start(f32[128,128,32]{1,2,0:T(8,128)} %fusion.87) | copy-start | bytes 6291460
  149.0 16.3 %copy-start.3 = (f32[128,128,32]{1,2,0:T(8,128)S(1)}, f32[128,128,32]{1,2,0:T(8,128)}, u32[]{:S(2)}) copy-start(f32[128,128,32]{1,2,0:T(8,128)} %fusion.85) | copy-start | bytes 6291460
  153.4 12.0 %copy-start.2 = (f32[128,128,32]{1,2,0:T(8,128)S(1)}, f32[128,128,32]{1,2,0:T(8,128)}, u32[]{:S(2)}) copy-start(f32[128,128,32]{1,2,0:T(8,128)} %fusion.83) | copy-start | bytes 6291460
  155.6 9.8 %copy-start = (f32[128,128,32]{1,2,0:T(8,128)S(1)}, f32[128,128,32]{1,2,0:T(8,128)}, u32[]{:S(2)}) copy-start(f32[128,128,32]{1,2,0:T(8,128)} %fusion.79) | copy-start | bytes 6291460
  155.6 9.8 %copy-start.1 = (f32[128,128,32]{1,2,0:T(8,128)S(1)}, f32[128,128,32]{1,2,0:T(8,128)}, u32[]{:S(2)}) copy-start(f32[128,128,32]{1,2,0:T(8,128)} %fusion.81) | copy-start | bytes 6291460
  155.6 9.8 %copy-start.11 = (f32[32]{0:T(128)S(1)}, f32[32]{0:T(128)}, u32[]{:S(2)}) copy-start(f32[32]{0:T(128)} %param.16) | copy-start | bytes 388
  162.3 7.3 %collective-permute-start.5 = (bf16[128,2,128]{2,1,0:T(2,128)(2,1)S(1)}, bf16[128,2,128]{2,1,0:T(2,128)(2,1)S(1)}, u32[]{:S(2)}, u32[]{:S(2)}) collective-permute-start(bf16[128,2,128]{2,1,0:T(2,128)(2,1)S(1)} %bitcast.290), channel_id=1, source_target_pairs={{4,0},{8,4},{12,8},{16,12},{20,16},{24,20},{28,24},{5,1},{9,5},{13... | collective-permute-start | bytes 196616 | tf_op jit(solution)/shard_map/ppermute | solution.py:11
where the time goes:
time: 181 us; the launch traced here: 180 us
  matrix products  124 us (69%)
  starting transfers between devices  19.9 us (11%)
  blocking collectives  13.8 us (8%)
  local copies, waits for them, and re-layouts  9.63 us (5%)
  other arithmetic  7.78 us (4%)
  waiting for transfers between devices  3.59 us (2%)
    dot_general x18, matrix products, conv_back(): jnp.einsum('oi,xoy->xiy', weights[shift_row, shift_col], window, preferre...  59.7 us
    dot_general x18, matrix products, conv_valid(): jnp.einsum('oi,xiy->xoy', weights[shift_row, shift_col], window, preferre...  55.9 us
    ppermute x2, starting transfers between devices, with_halo(): lax.ppermute(lax.slice_in_dim(block, block.shape[dim] - width, None, axis...  8.54 us
    all_gather x1, blocking collectives, shards(): shard_piece = lax.all_gather(both_halves, 'col', axis=0, tiled=True)  7.48 us
    all_gather x1, blocking collectives, shards(): shard_piece = lax.all_gather(packed, 'col', axis=0, tiled=True)  6.3 us
    ppermute x2, starting transfers between devices, from_behind(): return lax.ppermute(x, axis, pairs)  6.19 us
    ppermute x2, starting transfers between devices, with_halo(): lax.ppermute(lax.slice_in_dim(block, 0, width, axis=dim), axis, backward)  5.17 us
    dot_general x4, matrix products, column_block(): jnp.einsum('pk,phr->khr', pin_cols, pin_factor, preferred_element_type=jn...  4.31 us
  transfers between devices with their start and end apart: 6, of which 3 were waited for; matrix products, arithmetic and copies ran while one was open for 4% of the time, Pallas kernels for 0%

commit v1 on v0

--- a/solution.py
+++ b/solution.py
@@ -157,7 +157,22 @@
     both_halves = jnp.stack([back_maps, from_below], axis=1).reshape(tile_cols, 4 * span)
     left_col = net_box[:, 0]
     right_col = net_box[:, 1]
-    shard_piece = lax.all_gather(both_halves, "col", axis=0, tiled=True)
+    ways, here, step = (lax.axis_size("col"), lax.axis_index("col"), both_halves.shape[0])
+    shape = [n * ways if d == 0 else n for d, n in enumerate(both_halves.shape)]
+    shard_piece = lax.dynamic_update_slice_in_dim(
+        jnp.zeros(shape, both_halves.dtype), both_halves, here * step, axis=0
+    )
+    going_up = going_down = both_halves
+    for far in range(1, ways // 2 + 1):
+        going_up = lax.ppermute(going_up, "col", [(d, (d + 1) % ways) for d in range(ways)])
+        shard_piece = lax.dynamic_update_slice_in_dim(
+            shard_piece, going_up, (here - far) % ways * step, axis=0
+        )
+        if 2 * far < ways:
+            going_down = lax.ppermute(going_down, "col", [(d, (d - 1) % ways) for d in range(ways)])
+            shard_piece = lax.dynamic_update_slice_in_dim(
+                shard_piece, going_down, (here + far) % ways * step, axis=0
+            )
     piece_cols = jnp.arange(shard_piece.shape[0], dtype=jnp.int32)
     net_cols = (
         (left_col[:, None] <= piece_cols[None, :]) & (piece_cols[None, :] <= right_col[:, None])

time: 181 us -> 177 us (0.978)
  waiting for transfers between devices: 3.59 us -> 13.5 us
  matrix products: 124 us -> 116 us
  blocking collectives: 13.8 us -> 6.3 us
    dot_general x18, matrix products: 59.7 us -> 49.3 us  [conv_back(): jnp.einsum('oi,xoy->xiy', weights[shift_row, shift_col], window, preferre...]
    all_gather x1 -> x0, blocking collectives: 7.48 us -> none  [shards(): shard_piece = lax.all_gather(both_halves, 'col', axis=0, tiled=True)]
    ppermute x2, waiting for transfers between devices: 0.45 us -> 6.56 us  [with_halo(): lax.ppermute(lax.slice_in_dim(block, 0, width, axis=dim), axis, backward)]
    ppermute x0 -> x3, starting transfers between devices: none -> 3 us  [the longest x2 2.99 us: shards(): lax.ppermute(going_up, 'col', [(d, (d + 1) % ways) for d in range(ways)])]
    ppermute x0 -> x3, waiting for transfers between devices: none -> 2.89 us  [the longest x1 2.89 us: shards(): lax.ppermute(going_down, 'col', [(d, (d - 1) % ways) for d in range(ways)])]
    dot_general x18, matrix products: 55.9 us -> 58.2 us  [conv_valid(): jnp.einsum('oi,xiy->xoy', weights[shift_row, shift_col], window, preferre...]
    ppermute x2, waiting for transfers between devices: 1.8 us -> 4 us  [from_behind(): return lax.ppermute(x, axis, pairs)]
  transfers between devices with their start and end apart: 6 -> 9, of which waited for: 3 -> 5; matrix products, arithmetic and copies ran while one was open for 4% -> 6% of each run, Pallas kernels for 0% -> 0%
where the time goes in v1:
time: 177 us; the launch traced here: 176 us
  matrix products  116 us (66%)
  starting transfers between devices  21.7 us (12%)
  waiting for transfers between devices  13.5 us (8%)
  local copies, waits for them, and re-layouts  9.78 us (6%)
  other arithmetic  7.78 us (4%)
  blocking collectives  6.3 us (4%)
    dot_general x18, matrix products, conv_valid(): jnp.einsum('oi,xiy->xoy', weights[shift_row, shift_col], window, preferre...  58.2 us
    dot_general x18, matrix products, conv_back(): jnp.einsum('oi,xoy->xiy', weights[shift_row, shift_col], window, preferre...  49.3 us
    ppermute x2, starting transfers between devices, with_halo(): lax.ppermute(lax.slice_in_dim(block, block.shape[dim] - width, None, axis...  9.5 us
    ppermute x2, waiting for transfers between devices, with_halo(): lax.ppermute(lax.slice_in_dim(block, 0, width, axis=dim), axis, backward)  6.56 us
    all_gather x1, blocking collectives, shards(): shard_piece = lax.all_gather(packed, 'col', axis=0, tiled=True)  6.3 us
    ppermute x2, starting transfers between devices, from_behind(): return lax.ppermute(x, axis, pairs)  5.23 us
    dot_general x4, matrix products, column_block(): jnp.einsum('pk,phr->khr', pin_cols, pin_factor, preferred_element_type=jn...  4.31 us
    ppermute x2, starting transfers between devices, with_halo(): lax.ppermute(lax.slice_in_dim(block, 0, width, axis=dim), axis, backward)  4.02 us
  transfers between devices with their start and end apart: 9, of which 5 were waited for; matrix products, arithmetic and copies ran while one was open for 6% of the time, Pallas kernels for 0%

profile of v1, /device:TPU:19, one launch (start us, length us, event | category | flops | bytes accessed | tf_op | source)
XLA Modules:
  0.0 176.3 jit_solution(8406529939283590441)
XLA Ops:
  0.6 0.8 convert_element_type.81
  1.5 0.7 convert_element_type.80
  2.2 0.7 pad_maximum_fusion.10
  2.9 6.3 %all_gather.3 = f32[4096,13]{0,1:T(8,128)S(1)} all-gather(f32[1024,13]{0,1:T(8,128)S(1)} %pad_maximum_fusion.10), channel_id=1, replica_groups=mesh['strip'=8,'col'=4] {'col'}, dimensions={0}, use_global_device_ids=true | all-gather | bytes 266240 | tf_op jit(solution)/shard_map/all_gather | solution.py:112
  9.4 13.7 %while.11 = (s32[]{:T(128)}, f32[128,2,3,128]{3,0,2,1:T(8,128)S(1)}, f32[4,1024,13]{1,0,2:T(4,128)S(1)}, s32[]{:T(128)}, s32[]{:T(128)}, /*index=5*/s32[]{:T(128)}, s32[]{:T(128)}) while((s32[]{:T(128)}, f32[128,2,3,128]{3,0,2,1:T(8,128)S(1)}, f32[4,1024,13]{1,0,2:T(4,128)S(1)}, s32[]{:T(128)}, s32[]{:T(128)}, ...), condition=%wide.region_1.2_spmd.clone, body=%wide.region_0.1_spmd.clone.sunk | while | flops 408091520 | bytes 3318371 | solution.py:134
  9.9 0.5 fusion.254
  11.6 1.1 fusion.251
  13.4 0.5 fusion.254
  15.0 1.1 fusion.251
  16.8 0.5 fusion.254
  18.4 1.1 fusion.251
  20.2 0.5 fusion.254
  21.9 1.1 fusion.251
  23.3 3.2 %collective-permute-start = (bf16[128,3,128]{0,2,1:T(8,128)(2,1)S(1)}, bf16[128,3,128]{0,2,1:T(8,128)(2,1)S(1)}, u32[]{:S(2)}, u32[]{:S(2)}) collective-permute-start(bf16[128,3,128]{0,2,1:T(8,128)(2,1)S(1)} %fusion.144), channel_id=1, source_target_pairs={{0,4},{4,8},{8,12},{12,16},{16,20},{20,24},{24,28},{1,5},{5,9},{9,... | collective-permute-start | bytes 294920 | tf_op jit(solution)/shard_map/ppermute | solution.py:11
  26.6 1.0 copy.57
  27.6 1.8 %collective-permute-done = bf16[128,3,128]{0,2,1:T(8,128)(2,1)S(1)} collective-permute-done((bf16[128,3,128]{0,2,1:T(8,128)(2,1)S(1)}, bf16[128,3,128]{0,2,1:T(8,128)(2,1)S(1)}, u32[]{:S(2)}, u32[]{:S(2)}) %collective-permute-start) | collective-permute-done | bytes 98336 | tf_op jit(solution)/shard_map/ppermute | solution.py:11
  29.5 4.1 %collective-permute-start.1 = (bf16[128,35,2]{0,2,1:T(2,128)(2,1)S(1)}, bf16[128,35,2]{0,2,1:T(2,128)(2,1)S(1)}, u32[]{:S(2)}, u32[]{:S(2)}) collective-permute-start(bf16[128,35,2]{0,2,1:T(2,128)(2,1)S(1)} %get-tuple-element.86), channel_id=1, source_target_pairs={{0,4},{4,8},{8,12},{12,16},{16,20},{20,24},{24,28},{1,5},{5,9},{9,... | collective-permute-start | bytes 53768 | tf_op jit(solution)/shard_map/ppermute | solution.py:19
  33.6 1.9 %collective-permute-start.2 = (bf16[128,35,2]{0,2,1:T(2,128)(2,1)S(1)}, bf16[128,35,2]{0,2,1:T(2,128)(2,1)S(1)}, u32[]{:S(2)}, u32[]{:S(2)}) collective-permute-start(bf16[128,35,2]{0,2,1:T(2,128)(2,1)S(1)} %get-tuple-element.87), channel_id=1, source_target_pairs={{4,0},{8,4},{12,8},{16,12},{20,16},{24,20},{28,24},{5,1},{9,5},{13... | collective-permute-start | bytes 53768 | tf_op jit(solution)/shard_map/ppermute | solution.py:22
  35.5 3.4 %collective-permute-done.2 = bf16[128,35,2]{0,2,1:T(2,128)(2,1)S(1)} collective-permute-done((bf16[128,35,2]{0,2,1:T(2,128)(2,1)S(1)}, bf16[128,35,2]{0,2,1:T(2,128)(2,1)S(1)}, u32[]{:S(2)}, u32[]{:S(2)}) %collective-permute-start.2) | collective-permute-done | bytes 17952 | tf_op jit(solution)/shard_map/ppermute | solution.py:22
  39.0 1.6 pad_maximum_fusion.8
  40.6 3.6 %copy.58 = bf16[128,35,132]{2,1,0:T(8,128)(2,1)S(1)} copy(bf16[128,35,132]{0,2,1:T(8,128)(2,1)} %pad_maximum_fusion.8) | data formatting | bytes 2365440 | tf_op jit(solution)/shard_map/concatenate | solution.py:23
  44.2 5.4 %collective-permute-start.3 = (bf16[2,35,132]{2,1,0:T(8,128)(2,1)S(1)}, bf16[2,35,132]{2,1,0:T(8,128)(2,1)S(1)}, u32[]{:S(2)}, u32[]{:S(2)}) collective-permute-start(bf16[2,35,132]{2,1,0:T(8,128)(2,1)S(1)} %get-tuple-element.84), channel_id=1, source_target_pairs={{0,1},{1,2},{2,3},{4,5},{5,6},{6,7},{8,9},{9,10},{10,11},{12,13},{... | collective-permute-start | bytes 55448 | tf_op jit(solution)/shard_map/ppermute | solution.py:19
  49.7 2.1 %collective-permute-start.4 = (bf16[2,35,132]{2,1,0:T(8,128)(2,1)S(1)}, bf16[2,35,132]{2,1,0:T(8,128)(2,1)S(1)}, u32[]{:S(2)}, u32[]{:S(2)}) collective-permute-start(bf16[2,35,132]{2,1,0:T(8,128)(2,1)S(1)} %get-tuple-element.85), channel_id=1, source_target_pairs={{1,0},{2,1},{3,2},{5,4},{6,5},{7,6},{9,8},{10,9},{11,10},{13,12},{... | collective-permute-start | bytes 55448 | tf_op jit(solution)/shard_map/ppermute | solution.py:22
  51.9 3.1 %collective-permute-done.4 = bf16[2,35,132]{2,1,0:T(8,128)(2,1)S(1)} collective-permute-done((bf16[2,35,132]{2,1,0:T(8,128)(2,1)S(1)}, bf16[2,35,132]{2,1,0:T(8,128)(2,1)S(1)}, u32[]{:S(2)}, u32[]{:S(2)}) %collective-permute-start.4) | collective-permute-done | bytes 18512 | tf_op jit(solution)/shard_map/ppermute | solution.py:22
  55.0 0.6 pad_maximum_fusion.1
  55.5 2.7 %fusion.51 = f32[130,130,32]{1,2,0:T(8,128)} fusion(bf16[132,35,132]{2,1,0:T(8,128)(2,1)S(1)} %pad_maximum_fusion.1, bf16[3,3,32,32]{3,2,1,0:T(8,128)(2,1)S(1)} %copy-done.4), kind=kOutput, calls=%fused_computation.68 | convolution fusion | flops 34611200 | bytes 4301312 | tf_op jit(solution)/shard_map/oi,xoy->xiy/dot_general | solution.py:56
  58.3 3.2 %fusion.55 = f32[130,130,32]{1,2,0:T(8,128)} fusion(bf16[132,35,132]{2,1,0:T(8,128)(2,1)S(1)} %pad_maximum_fusion.1, bf16[3,3,32,32]{3,2,1,0:T(8,128)(2,1)S(1)} %copy-done.4), kind=kOutput, calls=%fused_computation.73 | convolution fusion | flops 34611200 | bytes 4301312 | tf_op jit(solution)/shard_map/oi,xoy->xiy/dot_general | solution.py:56
  61.5 3.2 %fusion.57 = f32[130,130,32]{1,2,0:T(8,128)} fusion(bf16[132,35,132]{2,1,0:T(8,128)(2,1)S(1)} %pad_maximum_fusion.1, bf16[3,3,32,32]{3,2,1,0:T(8,128)(2,1)S(1)} %copy-done.4), kind=kOutput, calls=%fused_computation.75 | convolution fusion | flops 34611200 | bytes 4301312 | tf_op jit(solution)/shard_map/oi,xoy->xiy/dot_general | solution.py:56
  64.8 2.8 %fusion.132 = f32[130,130,32]{1,2,0:T(8,128)} fusion(bf16[2,35,132]{2,1,0:T(8,128)(2,1)S(1)} %collective-permute-done.4, bf16[128,35,132]{2,1,0:T(8,128)(2,1)S(1)} %copy.58, bf16[2,35,132]{2,1,0:T(8,128)(2,1)S(1)} %collective-permute-done.3, bf16[3,3,32,3]{2,3,1,0:T(4,128)(2,1)S(1)} %copy-done.6), kind=kOutput, calls=%fused_computation.161 | convolution fusion | flops 3549000 | bytes 4867584 | tf_op jit(solution)/shard_map/oi,xiy->xoy/dot_general | solution.py:37
  67.6 2.9 %fusion.118 = f32[130,130,32]{1,2,0:T(8,128)} fusion(bf16[2,35,132]{2,1,0:T(8,128)(2,1)S(1)} %collective-permute-done.4, bf16[128,35,132]{2,1,0:T(8,128)(2,1)S(1)} %copy.58, bf16[2,35,132]{2,1,0:T(8,128)(2,1)S(1)} %collective-permute-done.3, bf16[3,3,32,3]{2,3,1,0:T(4,128)(2,1)S(1)} %copy-done.6), kind=kOutput, calls=%fused_computation.147 | convolution fusion | flops 3549000 | bytes 4867584 | tf_op jit(solution)/shard_map/oi,xiy->xoy/dot_general | solution.py:37
  70.4 2.8 %fusion.114 = f32[130,130,32]{1,2,0:T(8,128)} fusion(bf16[2,35,132]{2,1,0:T(8,128)(2,1)S(1)} %collective-permute-done.4, bf16[128,35,132]{2,1,0:T(8,128)(2,1)S(1)} %copy.58, bf16[3,3,32,3]{2,3,1,0:T(4,128)(2,1)S(1)} %copy-done.6), kind=kOutput, calls=%fused_computation.143 | convolution fusion | flops 3447600 | bytes 4826624 | tf_op jit(solution)/shard_map/oi,xiy->xoy/dot_general | solution.py:37
  73.2 2.7 %fusion.124 = f32[130,130,32]{1,2,0:T(8,128)} fusion(bf16[128,35,132]{2,1,0:T(8,128)(2,1)S(1)} %copy.58, bf16[2,35,132]{2,1,0:T(8,128)(2,1)S(1)} %collective-permute-done.3, bf16[3,3,32,3]{2,3,1,0:T(4,128)(2,1)S(1)} %copy-done.6), kind=kOutput, calls=%fused_computation.153 | convolution fusion | flops 3447600 | bytes 4826624 | tf_op jit(solution)/shard_map/oi,xiy->xoy/dot_general | solution.py:37
  76.0 2.9 %fusion.128 = f32[130,130,32]{1,2,0:T(8,128)} fusion(bf16[2,35,132]{2,1,0:T(8,128)(2,1)S(1)} %collective-permute-done.4, bf16[128,35,132]{2,1,0:T(8,128)(2,1)S(1)} %copy.58, bf16[3,3,32,3]{2,3,1,0:T(4,128)(2,1)S(1)} %copy-done.6), kind=kOutput, calls=%fused_computation.157 | convolution fusion | flops 3447600 | bytes 4826624 | tf_op jit(solution)/shard_map/oi,xiy->xoy/dot_general | solution.py:37
  78.8 2.7 %fusion.138 = f32[130,130,32]{1,2,0:T(8,128)} fusion(bf16[128,35,132]{2,1,0:T(8,128)(2,1)S(1)} %copy.58, bf16[2,35,132]{2,1,0:T(8,128)(2,1)S(1)} %collective-permute-done.3, bf16[3,3,32,3]{2,3,1,0:T(4,128)(2,1)S(1)} %copy-done.6), kind=kOutput, calls=%fused_computation.167 | convolution fusion | flops 3447600 | bytes 4826624 | tf_op jit(solution)/shard_map/oi,xiy->xoy/dot_general | solution.py:37
  81.6 2.8 %fusion.110 = f32[130,130,32]{1,2,0:T(8,128)} fusion(bf16[128,35,132]{2,1,0:T(8,128)(2,1)S(1)} %copy.58, bf16[2,35,132]{2,1,0:T(8,128)(2,1)S(1)} %collective-permute-done.3, bf16[3,3,32,3]{2,3,1,0:T(4,128)(2,1)S(1)} %copy-done.6), kind=kOutput, calls=%fused_computation.139 | convolution fusion | flops 3447600 | bytes 4826624 | tf_op jit(solution)/shard_map/oi,xiy->xoy/dot_general | solution.py:37
  84.3 2.7 %fusion.104 = f32[130,130,32]{1,2,0:T(8,128)} fusion(bf16[2,35,132]{2,1,0:T(8,128)(2,1)S(1)} %collective-permute-done.4, bf16[128,35,132]{2,1,0:T(8,128)(2,1)S(1)} %copy.58, bf16[2,35,132]{2,1,0:T(8,128)(2,1)S(1)} %collective-permute-done.3, bf16[3,3,32,3]{2,3,1,0:T(4,128)(2,1)S(1)} %copy-done.6), kind=kOutput, calls=%fused_computation.133 | convolution fusion | flops 3549000 | bytes 4867584 | tf_op jit(solution)/shard_map/oi,xiy->xoy/dot_general | solution.py:37
  87.1 12.9 %fusion.34 = (bf16[130,32,130]{2,1,0:T(8,128)(2,1)S(1)}, f32[130,130,32]{1,2,0:T(8,128)S(1)}) fusion(pred[130,130]{1,0:T(8,128)(4,1)S(1)} %broadcast_and_fusion, f32[32]{0:T(128)S(1)} %copy-done.8, bf16[3,3,32,3]{2,3,1,0:T(4,128)(2,1)S(1)} %copy-done.6, bf16[2,35,132]{2,1,0:T(8,128)(2,1)S(1)} %collective-permute-done.4, ...), kind=kOutput, calls=%fused_computation.44 | convolution fusion | flops 11559600 | bytes 23249152 | tf_op jit(solution)/shard_map/oi,xiy->xoy/dot_general | solution.py:37
  100.0 2.0 %fusion.79 = f32[128,128,32]{1,2,0:T(8,128)} fusion(bf16[130,32,130]{2,1,0:T(8,128)(2,1)S(1)} %get-tuple-element.92, bf16[3,3,32,32]{3,2,1,0:T(8,128)(2,1)S(1)} %copy-done.4), kind=kOutput, calls=%fused_computation.110 | convolution fusion | flops 33554432 | bytes 3153920 | tf_op jit(solution)/shard_map/oi,xiy->xoy/dot_general | solution.py:37
  102.1 1.9 %fusion.81 = f32[128,128,32]{1,2,0:T(8,128)} fusion(bf16[130,32,130]{2,1,0:T(8,128)(2,1)S(1)} %get-tuple-element.92, bf16[3,3,32,32]{3,2,1,0:T(8,128)(2,1)S(1)} %copy-done.4), kind=kOutput, calls=%fused_computation.112 | convolution fusion | flops 33554432 | bytes 3153920 | tf_op jit(solution)/shard_map/oi,xiy->xoy/dot_general | solution.py:37
  103.9 1.9 %fusion.83 = f32[128,128,32]{1,2,0:T(8,128)} fusion(bf16[130,32,130]{2,1,0:T(8,128)(2,1)S(1)} %get-tuple-element.92, bf16[3,3,32,32]{3,2,1,0:T(8,128)(2,1)S(1)} %copy-done.4), kind=kOutput, calls=%fused_computation.114 | convolution fusion | flops 33554432 | bytes 3153920 | tf_op jit(solution)/shard_map/oi,xiy->xoy/dot_general | solution.py:37
  105.8 1.9 %fusion.85 = f32[128,128,32]{1,2,0:T(8,128)} fusion(bf16[130,32,130]{2,1,0:T(8,128)(2,1)S(1)} %get-tuple-element.92, bf16[3,3,32,32]{3,2,1,0:T(8,128)(2,1)S(1)} %copy-done.4), kind=kOutput, calls=%fused_computation.116 | convolution fusion | flops 33554432 | bytes 3153920 | tf_op jit(solution)/shard_map/oi,xiy->xoy/dot_general | solution.py:37
  107.7 1.9 %fusion.87 = f32[128,128,32]{1,2,0:T(8,128)} fusion(bf16[130,32,130]{2,1,0:T(8,128)(2,1)S(1)} %get-tuple-element.92, bf16[3,3,32,32]{3,2,1,0:T(8,128)(2,1)S(1)} %copy-done.4), kind=kOutput, calls=%fused_computation.118 | convolution fusion | flops 33554432 | bytes 3153920 | tf_op jit(solution)/shard_map/oi,xiy->xoy/dot_general | solution.py:37
  109.6 1.7 fusion.89
  111.3 1.7 fusion.91
  113.0 3.7 %fusion.38 = f32[130,130,32]{1,2,0:T(8,128)} fusion(bf16[128,35,132]{2,1,0:T(8,128)(2,1)S(1)} %copy.58, bf16[2,35,132]{2,1,0:T(8,128)(2,1)S(1)} %collective-permute-done.4, bf16[3,3,32,32]{3,2,1,0:T(8,128)(2,1)S(1)} %copy-done.4), kind=kOutput, calls=%fused_computation.58 | convolution fusion | flops 35152000 | bytes 4833792 | tf_op jit(solution)/shard_map/oi,xoy->xiy/dot_general | solution.py:56
  116.7 3.6 %fusion.41 = f32[130,130,32]{1,2,0:T(8,128)} fusion(bf16[128,35,132]{2,1,0:T(8,128)(2,1)S(1)} %copy.58, bf16[2,35,132]{2,1,0:T(8,128)(2,1)S(1)} %collective-permute-done.4, bf16[3,3,32,32]{3,2,1,0:T(8,128)(2,1)S(1)} %copy-done.4), kind=kOutput, calls=%fused_computation.60 | convolution fusion | flops 35152000 | bytes 4833792 | tf_op jit(solution)/shard_map/oi,xoy->xiy/dot_general | solution.py:56
  120.3 3.6 %fusion.44 = f32[130,130,32]{1,2,0:T(8,128)} fusion(bf16[128,35,132]{2,1,0:T(8,128)(2,1)S(1)} %copy.58, bf16[2,35,132]{2,1,0:T(8,128)(2,1)S(1)} %collective-permute-done.3, bf16[3,3,32,32]{3,2,1,0:T(8,128)(2,1)S(1)} %copy-done.4), kind=kOutput, calls=%fused_computation.62 | convolution fusion | flops 35152000 | bytes 4833792 | tf_op jit(solution)/shard_map/oi,xoy->xiy/dot_general | solution.py:56
  123.9 3.7 %fusion.47 = f32[130,130,32]{1,2,0:T(8,128)} fusion(bf16[128,35,132]{2,1,0:T(8,128)(2,1)S(1)} %copy.58, bf16[2,35,132]{2,1,0:T(8,128)(2,1)S(1)} %collective-permute-done.3, bf16[3,3,32,32]{3,2,1,0:T(8,128)(2,1)S(1)} %copy-done.4), kind=kOutput, calls=%fused_computation.64 | convolution fusion | flops 35152000 | bytes 4833792 | tf_op jit(solution)/shard_map/oi,xoy->xiy/dot_general | solution.py:56
  127.6 2.7 %fusion.53 = f32[130,130,32]{1,2,0:T(8,128)} fusion(bf16[2,35,132]{2,1,0:T(8,128)(2,1)S(1)} %collective-permute-done.4, bf16[128,35,132]{2,1,0:T(8,128)(2,1)S(1)} %copy.58, bf16[3,3,32,32]{3,2,1,0:T(8,128)(2,1)S(1)} %copy-done.4), kind=kOutput, calls=%fused_computation.71 | convolution fusion | flops 36774400 | bytes 4833792 | tf_op jit(solution)/shard_map/oi,xoy->xiy/dot_general | solution.py:56
  130.4 14.0 %fusion.29 = bf16[130,32,130]{2,1,0:T(8,128)(2,1)} fusion(f32[130,130,32]{1,2,0:T(8,128)S(1)} %get-tuple-element.93, f32[130,130,32]{1,2,0:T(8,128)} %fusion.51, f32[130,130,32]{1,2,0:T(8,128)} %fusion.53, f32[130,130,32]{1,2,0:T(8,128)} %fusion.44, f32[130,130,32]{1,2,0:T(8,128)} %fusion.55, f32[130,130,32]{1,2,0:T(8,128)} %fusion.38, ...), kind=kOutput, calls=%fused_computation.36 | convolution fusion | flops 46508800 | bytes 25352448 | tf_op jit(solution)/shard_map/oi,xoy->xiy/dot_general | solution.py:56
  144.4 2.2 %fusion.76 = f32[128,128,2]{1,2,0:T(2,128)S(1)} fusion(bf16[130,32,130]{2,1,0:T(8,128)(2,1)} %fusion.29, bf16[3,3,32,3]{2,3,1,0:T(4,128)(2,1)S(1)} %copy-done.6), kind=kOutput, calls=%fused_computation.107 | convolution fusion | flops 2097152 | bytes 1180160 | tf_op jit(solution)/shard_map/oi,xoy->xiy/dot_general | solution.py:56
  146.7 2.1 %convolution_add_fusion.7 = f32[128,128,2]{1,2,0:T(2,128)S(1)} fusion(f32[128,128,2]{1,2,0:T(2,128)S(1)} %fusion.76, bf16[130,32,130]{2,1,0:T(8,128)(2,1)} %fusion.29, bf16[3,3,32,3]{2,3,1,0:T(4,128)(2,1)S(1)} %copy-done.6), kind=kOutput, calls=%fused_computation.91 | convolution fusion | flops 2129920 | bytes 1311232 | tf_op jit(solution)/shard_map/oi,xoy->xiy/dot_general | solution.py:56
  148.7 2.1 %convolution_add_fusion.6 = f32[128,128,2]{1,2,0:T(2,128)S(1)} fusion(f32[128,128,2]{1,2,0:T(2,128)S(1)} %convolution_add_fusion.7, bf16[130,32,130]{2,1,0:T(8,128)(2,1)} %fusion.29, bf16[3,3,32,3]{2,3,1,0:T(4,128)(2,1)S(1)} %copy-done.6), kind=kOutput, calls=%fused_computation.90 | convolution fusion | flops 2129920 | bytes 1311232 | tf_op jit(solution)/shard_map/oi,xoy->xiy/dot_general | solution.py:56
  150.8 0.5 convolution_add_fusion.5
  151.3 0.5 convolution_add_fusion.4
  153.1 2.1 %collective-permute-start.5 = (bf16[128,2,128]{2,1,0:T(2,128)(2,1)S(1)}, bf16[128,2,128]{2,1,0:T(2,128)(2,1)S(1)}, u32[]{:S(2)}, u32[]{:S(2)}) collective-permute-start(bf16[128,2,128]{2,1,0:T(2,128)(2,1)S(1)} %bitcast.292), channel_id=1, source_target_pairs={{4,0},{8,4},{12,8},{16,12},{20,16},{24,20},{28,24},{5,1},{9,5},{13... | collective-permute-start | bytes 196616 | tf_op jit(solution)/shard_map/ppermute | solution.py:11
  155.2 1.8 %fusion.93 = f32[128,128,32]{1,2,0:T(8,128)} fusion(bf16[130,32,130]{2,1,0:T(8,128)(2,1)S(1)} %get-tuple-element.92, bf16[3,3,32,32]{3,2,1,0:T(8,128)(2,1)S(1)} %copy-done.4), kind=kOutput, calls=%fused_computation.124 | convolution fusion | flops 33554432 | bytes 3153920 | tf_op jit(solution)/shard_map/oi,xiy->xoy/dot_general | solution.py:37
  157.0 2.2 %collective-permute-done.5 = bf16[128,2,128]{2,1,0:T(2,128)(2,1)S(1)} collective-permute-done((bf16[128,2,128]{2,1,0:T(2,128)(2,1)S(1)}, bf16[128,2,128]{2,1,0:T(2,128)(2,1)S(1)}, u32[]{:S(2)}, u32[]{:S(2)}) %collective-permute-start.5) | collective-permute-done | bytes 65568 | tf_op jit(solution)/shard_map/ppermute | solution.py:11
  159.5 1.2 collective-permute-start.6
  160.7 8.2 %fusion.62 = bf16[128,32,128]{2,1,0:T(8,128)(2,1)} fusion(f32[128,128,32]{1,2,0:T(8,128)S(1)} %copy-done.1, f32[128,128,32]{1,2,0:T(8,128)} %fusion.81, f32[128,128,32]{1,2,0:T(8,128)} %fusion.83, f32[128,128,32]{1,2,0:T(8,128)} %fusion.85, f32[128,128,32]{1,2,0:T(8,128)} %fusion.87, f32[128,128,32]{1,2,0:T(8,128)} %fusion.89, f32[128,128,32]{1,2,0:T(8,128)} %fusion.93, ...), kind=kOutput, calls=%fused_computation.82 | convolution fusion | flops 38797312 | bytes 18883072 | tf_op jit(solution)/shard_map/oi,xiy->xoy/dot_general | solution.py:37
  169.0 1.8 %collective-permute-start.8 = (bf16[128,512]{0,1:T(8,128)(2,1)S(1)}, bf16[128,512]{0,1:T(8,128)(2,1)S(1)}, u32[]{:S(2)}, u32[]{:S(2)}) collective-permute-start(bf16[128,512]{0,1:T(8,128)(2,1)S(1)} %collective-permute-done.6), channel_id=1, source_target_pairs={{0,1},{1,2},{2,3},{3,0},{4,5},{5,6},{6,7},{7,4},{8,9},{9,10},{10,1... | collective-permute-start | bytes 393224 | tf_op jit(solution)/shard_map/ppermute | solution.py:167
  170.8 2.9 %collective-permute-done.7 = bf16[128,512]{0,1:T(8,128)(2,1)S(1)} collective-permute-done((bf16[128,512]{0,1:T(8,128)(2,1)S(1)}, bf16[128,512]{0,1:T(8,128)(2,1)S(1)}, u32[]{:S(2)}, u32[]{:S(2)}) %collective-permute-start.7) | collective-permute-done | bytes 131104 | tf_op jit(solution)/shard_map/ppermute | solution.py:172
  173.8 1.6 fusion.60
  175.4 0.9 fusion.97
  (115 shorter events, 9.0 us)
Async XLA Ops:
  9.3 17.2 %copy-start.5 = (s32[1024,4]{0,1:T(4,128)S(1)}, s32[1024,4]{0,1:T(4,128)}, u32[]{:S(2)}) copy-start(s32[1024,4]{0,1:T(4,128)} %param.10) | copy-start | bytes 49156
  9.3 17.3 %copy-start.3 = (bf16[128,32,128]{2,1,0:T(8,128)(2,1)S(1)}, bf16[128,32,128]{2,1,0:T(8,128)(2,1)}, u32[]{:S(2)}) copy-start(bf16[128,32,128]{2,1,0:T(8,128)(2,1)} %param.17) | copy-start | bytes 3145732
  23.3 6.1 %collective-permute-start = (bf16[128,3,128]{0,2,1:T(8,128)(2,1)S(1)}, bf16[128,3,128]{0,2,1:T(8,128)(2,1)S(1)}, u32[]{:S(2)}, u32[]{:S(2)}) collective-permute-start(bf16[128,3,128]{0,2,1:T(8,128)(2,1)S(1)} %fusion.144), channel_id=1, source_target_pairs={{0,4},{4,8},{8,12},{12,16},{16,20},{20,24},{24,28},{1,5},{5,9},{9,... | collective-permute-start | bytes 294920 | tf_op jit(solution)/shard_map/ppermute | solution.py:11
  29.5 6.0 %collective-permute-start.1 = (bf16[128,35,2]{0,2,1:T(2,128)(2,1)S(1)}, bf16[128,35,2]{0,2,1:T(2,128)(2,1)S(1)}, u32[]{:S(2)}, u32[]{:S(2)}) collective-permute-start(bf16[128,35,2]{0,2,1:T(2,128)(2,1)S(1)} %get-tuple-element.86), channel_id=1, source_target_pairs={{0,4},{4,8},{8,12},{12,16},{16,20},{20,24},{24,28},{1,5},{5,9},{9,... | collective-permute-start | bytes 53768 | tf_op jit(solution)/shard_map/ppermute | solution.py:19
  33.6 5.4 %collective-permute-start.2 = (bf16[128,35,2]{0,2,1:T(2,128)(2,1)S(1)}, bf16[128,35,2]{0,2,1:T(2,128)(2,1)S(1)}, u32[]{:S(2)}, u32[]{:S(2)}) collective-permute-start(bf16[128,35,2]{0,2,1:T(2,128)(2,1)S(1)} %get-tuple-element.87), channel_id=1, source_target_pairs={{4,0},{8,4},{12,8},{16,12},{20,16},{24,20},{28,24},{5,1},{9,5},{13... | collective-permute-start | bytes 53768 | tf_op jit(solution)/shard_map/ppermute | solution.py:22
  44.2 7.6 %collective-permute-start.3 = (bf16[2,35,132]{2,1,0:T(8,128)(2,1)S(1)}, bf16[2,35,132]{2,1,0:T(8,128)(2,1)S(1)}, u32[]{:S(2)}, u32[]{:S(2)}) collective-permute-start(bf16[2,35,132]{2,1,0:T(8,128)(2,1)S(1)} %get-tuple-element.84), channel_id=1, source_target_pairs={{0,1},{1,2},{2,3},{4,5},{5,6},{6,7},{8,9},{9,10},{10,11},{12,13},{... | collective-permute-start | bytes 55448 | tf_op jit(solution)/shard_map/ppermute | solution.py:19
  49.7 5.3 %collective-permute-start.4 = (bf16[2,35,132]{2,1,0:T(8,128)(2,1)S(1)}, bf16[2,35,132]{2,1,0:T(8,128)(2,1)S(1)}, u32[]{:S(2)}, u32[]{:S(2)}) collective-permute-start(bf16[2,35,132]{2,1,0:T(8,128)(2,1)S(1)} %get-tuple-element.85), channel_id=1, source_target_pairs={{1,0},{2,1},{3,2},{5,4},{6,5},{7,6},{9,8},{10,9},{11,10},{13,12},{... | collective-permute-start | bytes 55448 | tf_op jit(solution)/shard_map/ppermute | solution.py:22
  51.8 3.7 %copy-start.4 = (bf16[3,3,32,32]{3,2,1,0:T(8,128)(2,1)S(1)}, bf16[3,3,32,32]{3,2,1,0:T(8,128)(2,1)}, u32[]{:S(2)}) copy-start(bf16[3,3,32,32]{3,2,1,0:T(8,128)(2,1)} %param.15) | copy-start | bytes 55300
  61.5 3.2 %copy-start.6 = (bf16[3,3,32,3]{2,3,1,0:T(4,128)(2,1)S(1)}, bf16[3,3,32,3]{2,3,1,0:T(4,128)(2,1)}, u32[]{:S(2)}) copy-start(bf16[3,3,32,3]{2,3,1,0:T(4,128)(2,1)} %param.13) | copy-start | bytes 5188
  84.3 2.7 %copy-start.8 = (f32[32]{0:T(128)S(1)}, f32[32]{0:T(128)}, u32[]{:S(2)}) copy-start(f32[32]{0:T(128)} %param.14) | copy-start | bytes 388
  100.0 55.2 %copy-start = (bf16[130,32,130]{2,1,0:T(8,128)(2,1)}, bf16[130,32,130]{2,1,0:T(8,128)(2,1)S(1)}, u32[]{:S(2)}) copy-start(bf16[130,32,130]{2,1,0:T(8,128)(2,1)S(1)} %get-tuple-element.92) | copy-start | bytes 3244804
  144.4 6.4 %copy-start.2 = (bf16[130,32,130]{2,1,0:T(8,128)(2,1)S(1)}, bf16[130,32,130]{2,1,0:T(8,128)(2,1)}, u32[]{:S(2)}) copy-start(bf16[130,32,130]{2,1,0:T(8,128)(2,1)} %fusion.29) | copy-start | bytes 3244804
  152.9 7.8 %copy-start.1 = (f32[128,128,32]{1,2,0:T(8,128)S(1)}, f32[128,128,32]{1,2,0:T(8,128)}, u32[]{:S(2)}) copy-start(f32[128,128,32]{1,2,0:T(8,128)} %fusion.79) | copy-start | bytes 6291460
  152.9 7.8 %copy-start.7 = (f32[32]{0:T(128)S(1)}, f32[32]{0:T(128)}, u32[]{:S(2)}) copy-start(f32[32]{0:T(128)} %param.16) | copy-start | bytes 388
  153.1 6.0 %collective-permute-start.5 = (bf16[128,2,128]{2,1,0:T(2,128)(2,1)S(1)}, bf16[128,2,128]{2,1,0:T(2,128)(2,1)S(1)}, u32[]{:S(2)}, u32[]{:S(2)}) collective-permute-start(bf16[128,2,128]{2,1,0:T(2,128)(2,1)S(1)} %bitcast.292), channel_id=1, source_target_pairs={{4,0},{8,4},{12,8},{16,12},{20,16},{24,20},{28,24},{5,1},{9,5},{13... | collective-permute-start | bytes 196616 | tf_op jit(solution)/shard_map/ppermute | solution.py:11
  159.5 9.5 %collective-permute-start.6 = (bf16[128,512]{0,1:T(8,128)(2,1)S(1)}, bf16[128,512]{0,1:T(8,128)(2,1)S(1)}, u32[]{:S(2)}, u32[]{:S(2)}) collective-permute-start(bf16[128,512]{0,1:T(8,128)(2,1)S(1)} %bitcast.285), channel_id=1, source_target_pairs={{0,1},{1,2},{2,3},{3,0},{4,5},{5,6},{6,7},{7,4},{8,9},{9,10},{10,1... | collective-permute-start | bytes 393224 | tf_op jit(solution)/shard_map/ppermute | solution.py:167
  168.9 4.8 %collective-permute-start.7 = (bf16[128,512]{0,1:T(8,128)(2,1)S(1)}, bf16[128,512]{0,1:T(8,128)(2,1)S(1)}, u32[]{:S(2)}, u32[]{:S(2)}) collective-permute-start(bf16[128,512]{0,1:T(8,128)(2,1)S(1)} %bitcast.286), channel_id=1, source_target_pairs={{0,3},{1,0},{2,1},{3,2},{4,7},{5,4},{6,5},{7,6},{8,11},{9,8},{10,9... | collective-permute-start | bytes 393224 | tf_op jit(solution)/shard_map/ppermute | solution.py:172
  169.0 4.8 %collective-permute-start.8 = (bf16[128,512]{0,1:T(8,128)(2,1)S(1)}, bf16[128,512]{0,1:T(8,128)(2,1)S(1)}, u32[]{:S(2)}, u32[]{:S(2)}) collective-permute-start(bf16[128,512]{0,1:T(8,128)(2,1)S(1)} %collective-permute-done.6), channel_id=1, source_target_pairs={{0,1},{1,2},{2,3},{3,0},{4,5},{5,6},{6,7},{7,4},{8,9},{9,10},{10,1... | collective-permute-start | bytes 393224 | tf_op jit(solution)/shard_map/ppermute | solution.py:167
